TPU v7x, 256 devices: a whole 4x4x8 slice. The times are simulated.
256 devices in a mesh: net: 32 (over x, z), scen: 8 (over y, core).
Axes of the slice: x: 4, y: 4, z: 8, core: 2. Of those that a mesh axis runs over, the one named last changes fastest.
Arguments:
- arc_flows: float32 [256, 262144], P('scen', 'net'), may hold values from 0 to 1
- node_duals: float32 [256, 65536], P('scen', 'net'), may hold values from -6 to 6
- demand: float32 [256, 65536], P('scen', 'net'), may hold values from -6 to 6
- excess: float32 [256], P('scen'), may hold values from 0 to 0.5
- risk_duals: float32 [256], P('scen'), may hold values from 0.2 to 6
- threshold: float32 [1], replicated, may hold values from -2.5 to -1.5
- arc_costs: float32 [262144], P('net'), may hold values from 0.05 to 0.75
- local_blocks: bfloat16 [2048, 4, 128, 128], P('net'), may hold values from -0.125 to 0.125
- head_blocks: bfloat16 [2048, 128, 128], P('net'), may hold values from -0.125 to 0.125
- local_index: int32 [2048, 4], P('net'), may hold values from 0 to 15
- head_index: int32 [2048], P('net'), may hold values from 0 to 511, as said below
Outputs:
- flows_next: float32 [256, 262144], P('scen', 'net')
- duals_next: float32 [256, 65536], P('scen', 'net')
- excess_next: float32 [256], P('scen')
- risk_next: float32 [256], P('scen')
- threshold_next: float32 [1], replicated
Inputs may be any that keep to these rules, and one draw needn't show every extreme that they name: Among the arc blocks of one device, at most 4 have their head node block on any one device of net (head_index // 16 names the device), and in every device's arc blocks some device of net is named exactly 4 times.
All inputs are finite; a program needn't handle non-finite values.
Results may differ from a plain program's by a relative error of at most 0.0021.
Values may be sent and summed in bfloat16 or wider, within the bound.
A program may use at most 128 MiB of HBM per device.

v0:
```python
import jax
import jax.numpy as jnp
from jax import lax
from jax.sharding import PartitionSpec as P

ROUNDS = 3


primal_step = 0.5
dual_step = 0.5
risk_step = 1.0
tail_weight = 2.0


def per_device(
    arc_flows,
    node_duals,
    demand,
    excess,
    risk_duals,
    threshold,
    arc_costs,
    local_blocks,
    head_blocks,
    local_index,
    head_index,
):
    block_rows = local_blocks.shape[-1]
    scen_rows = arc_flows.shape[0]
    arc_blks = head_index.shape[0]
    node_blks = node_duals.shape[1] // block_rows
    touches = local_index.shape[1]
    net_size = lax.axis_size("net")
    scen_size = lax.axis_size("scen")
    slot_cap = max(2, (2 * arc_blks + net_size - 1) // net_size)
    slot_count = net_size * slot_cap
    arc_total = arc_flows.shape[1] * net_size
    scen_total = scen_rows * scen_size
    select_prec = lax.Precision.HIGH
    peer_dev = head_index // node_blks
    target = head_index % node_blks
    peer_hot = (peer_dev[:, None] == jnp.arange(net_size, dtype=jnp.int32)[None, :]).astype(
        jnp.int32
    )
    earlier = jnp.cumsum(peer_hot, axis=0) - peer_hot
    slot_rank = jnp.sum(earlier * peer_hot, axis=1)
    slot_ids = peer_dev * slot_cap + slot_rank
    slot_hot = slot_ids[:, None] == jnp.arange(slot_count, dtype=jnp.int32)[None, :]
    arc_ids = jnp.arange(arc_blks, dtype=jnp.int32)
    slot_arc = jnp.max(jnp.where(slot_hot, arc_ids[:, None], -1), axis=0)
    slot_filled = slot_arc >= 0
    slot_source = jnp.maximum(slot_arc, 0)
    wanted = jnp.max(jnp.where(slot_hot, target[:, None], -1), axis=0).reshape(net_size, slot_cap)
    asked = lax.all_to_all(wanted, "net", split_axis=0, concat_axis=0, tiled=True)
    asked_hot = asked.reshape(-1)[:, None] == jnp.arange(node_blks, dtype=jnp.int32)[None, :]
    local_hot = local_index[:, :, None] == jnp.arange(node_blks, dtype=jnp.int32)[None, None, :]
    asked_wide = asked_hot.astype(jnp.float32)
    local_wide = local_hot.astype(jnp.float32)
    local_half = local_hot.astype(jnp.bfloat16)
    flow_now = arc_flows
    dual_now = node_duals
    level = threshold
    excess_now = excess
    risk_now = risk_duals
    for iteration in range(ROUNDS):
        dual_panel = dual_now.astype(jnp.bfloat16)
        dual_grid = dual_panel.reshape(scen_rows, node_blks, block_rows)
        gathered = lax.all_gather(dual_panel, "net", axis=1, tiled=True)
        head_rows = jnp.take(gathered.reshape(scen_rows, -1, block_rows), head_index, axis=1)
        pull_summed = jnp.einsum(
            "sjn,jmn->sjm", head_rows, head_blocks, preferred_element_type=jnp.float32
        )
        for touched in range(touches):
            local_rows = jnp.einsum(
                "sbn,jb->sjn", dual_grid, local_half[:, touched], preferred_element_type=jnp.float32
            ).astype(jnp.bfloat16)
            pull_summed = pull_summed + jnp.einsum(
                "sjn,jmn->sjm",
                local_rows,
                local_blocks[:, touched],
                preferred_element_type=jnp.float32,
            )
        pulled = pull_summed.reshape(scen_rows, arc_blks * block_rows)
        risk_mine = risk_now
        mean_risk = lax.psum(jnp.sum(risk_now), "scen") / scen_total
        flows_new = jnp.maximum(
            flow_now - primal_step * (risk_mine[:, None] * arc_costs[None, :] - pulled), 0.0
        )
        level_new = level - primal_step * (1.0 - mean_risk)
        flows_bar = 2.0 * flows_new - flow_now
        level_bar = 2.0 * level_new - level
        partial_value = jnp.sum(arc_costs[None, :] * flows_bar, axis=1) / arc_total
        excess_new = jnp.maximum(excess_now - primal_step * (tail_weight - risk_now), 0.0)
        excess_bar = 2.0 * excess_new - excess_now
        losses = lax.psum(partial_value, "net")
        risk_now = jnp.maximum(risk_now + risk_step * (losses - excess_bar - level_bar), 0.0)
        excess_now = excess_new
        flow_grid = flows_bar.astype(jnp.bfloat16).reshape(scen_rows, arc_blks, block_rows)
        own_terms = jnp.einsum(
            "sjm,jmn->sjn", flow_grid, head_blocks, preferred_element_type=jnp.float32
        )
        term_pack = jnp.where(
            slot_filled[None, :, None], jnp.take(own_terms, slot_source, axis=1), 0.0
        )
        arrived = lax.all_to_all(
            term_pack.reshape(scen_rows, net_size, slot_cap, block_rows),
            "net",
            split_axis=1,
            concat_axis=1,
            tiled=True,
        )
        head_terms = arrived.reshape(scen_rows, slot_count, block_rows)
        summed = jnp.einsum("sqn,qb->sbn", head_terms, asked_wide, precision=select_prec)
        local_terms = jnp.einsum(
            "sjm,jkmn->sjkn", flow_grid, local_blocks, preferred_element_type=jnp.float32
        )
        summed = summed + jnp.einsum(
            "sjkn,jkb->sbn", local_terms, local_wide, precision=select_prec
        )
        dual_now = dual_now + dual_step * (
            demand - summed.reshape(scen_rows, node_blks * block_rows)
        )
        flow_now = flows_new
        level = level_new
    return (flow_now, dual_now, excess_now, risk_now, level)


def solution(mesh):
    placed = (
        P("scen", "net"),
        P("scen", "net"),
        P("scen", "net"),
        P("scen"),
        P("scen"),
        P(),
        P("net"),
        P("net", None, None, None),
        P("net", None, None),
        P("net", None),
        P("net"),
    )
    return jax.shard_map(
        per_device,
        mesh=mesh,
        in_specs=placed,
        out_specs=(P("scen", "net"), P("scen", "net"), P("scen"), P("scen"), P()),
        check_vma=False,
    )
```

profile of v0, /device:TPU:0, one launch (start us, length us, event | category | flops | bytes accessed | tf_op | source)
XLA Modules:
  0.0 596.9 jit_solution(4962526115088580452)
XLA Ops:
  7.2 1.8 convert_element_type.96
  10.9 9.6 %all-to-all-start = ((s32[32,1,4]{2,1,0:T(1,128)}), s32[32,1,4]{2,1,0:T(1,128)S(1)}, u32[]{:S(2)}, u32[]{:S(2)}) async-start(s32[32,1,4]{2,1,0:T(1,128)} %bitcast.20), calls=%async_computation | async-start | bytes 32768 | tf_op jit(solution)/shard_map/all_to_all | solution.py:54
  20.5 1.0 convert_bitcast_fusion
  23.9 1.1 fusion.87
  25.1 2.9 fusion.10
  27.9 3.8 fusion.16
  31.7 3.9 fusion.22
  35.6 58.6 %all-gather.4.cloned.1.call-done = bf16[32,65536]{1,0:T(8,128)(2,1)} async-done(((bf16[32,2048]{1,0:T(8,128)(2,1)}), bf16[32,65536]{1,0:T(8,128)(2,1)}) %all-gather.4.cloned.1.call-update) | async-done | bytes 4194320 | tf_op jit(solution)/shard_map/all_gather | solution.py:68
  94.2 4.9 copy_bitcast_fusion.2
  99.1 3.6 gather_fusion
  102.7 2.4 fusion.130
  105.2 3.0 fusion.54
  108.8 1.6 convolution_bitcast_fusion.5
  110.5 3.2 gather_fusion.1
  113.7 3.1 bitcast_select_fusion.2
  116.7 5.4 all-to-all-start.1
  123.7 1.3 fusion.215
  125.2 4.8 convolution_bitcast_fusion.2
  130.1 3.1 fusion.99
  133.2 37.1 %all-to-all-done.1 = f32[32,32,4,128]{3,0,2,1:T(8,128)} async-done(((f32[32,32,4,128]{3,0,2,1:T(8,128)}), f32[32,32,4,128]{3,0,2,1:T(8,128)}, u32[]{:S(2)}, u32[]{:S(2)}) %all-to-all-start.1) | async-done | bytes 2097184 | tf_op jit(solution)/shard_map/all_to_all | solution.py:105
  170.3 2.9 copy.120
  175.8 13.0 %psum.43 = f32[]{:T(128)} all-reduce(f32[]{:T(128)} %reduce_sum.64), channel_id=1, replica_groups=mesh['net'=32,'scen'=8] {'scen'}, use_global_device_ids=true, to_apply=%region_3.5 | all-reduce | flops 1 | bytes 8 | tf_op jit(solution)/shard_map/psum | solution.py:85
  190.2 72.2 %psum.42 = f32[32]{0:T(128)S(1)} all-reduce(f32[32]{0:T(128)S(1)} %broadcast_multiply_fusion.2), channel_id=1, replica_groups=mesh['net'=32,'scen'=8] {'net'}, use_global_device_ids=true, to_apply=%region_1.3 | all-reduce | flops 32 | bytes 256 | tf_op jit(solution)/shard_map/psum | solution.py:95
  263.0 0.9 copy.171
  265.0 1.2 fusion.91
  266.2 2.8 fusion.8
  269.0 3.9 fusion.14
  272.9 3.8 fusion.20
  276.6 4.9 copy_bitcast_fusion.1
  281.5 3.6 gather_fusion.2
  285.1 2.4 fusion.127
  287.6 3.0 fusion.69
  291.2 1.7 convolution_bitcast_fusion.4
  292.8 3.2 gather_fusion.3
  296.0 3.1 bitcast_select_fusion.1
  299.1 4.8 all-to-all-start.2
  304.4 1.3 fusion.213
  305.8 4.8 convolution_bitcast_fusion.1
  310.7 3.8 fusion.102
  314.5 25.8 %all-to-all-done.2 = f32[32,32,4,128]{3,0,2,1:T(8,128)} async-done(((f32[32,32,4,128]{3,0,2,1:T(8,128)}), f32[32,32,4,128]{3,0,2,1:T(8,128)}, u32[]{:S(2)}, u32[]{:S(2)}) %all-to-all-start.2) | async-done | bytes 2097184 | tf_op jit(solution)/shard_map/all_to_all | solution.py:105
  340.3 3.0 copy.130
  345.3 13.1 %psum.45 = f32[]{:T(128)} all-reduce(f32[]{:T(128)} %get-tuple-element.16), channel_id=1, replica_groups=mesh['net'=32,'scen'=8] {'scen'}, use_global_device_ids=true, to_apply=%region_11.14 | all-reduce | flops 1 | bytes 8 | tf_op jit(solution)/shard_map/psum | solution.py:85
  359.1 74.0 %psum.44 = f32[32]{0:T(128)S(1)} all-reduce(f32[32]{0:T(128)S(1)} %broadcast_multiply_fusion.1), channel_id=1, replica_groups=mesh['net'=32,'scen'=8] {'net'}, use_global_device_ids=true, to_apply=%region_9.12 | all-reduce | flops 32 | bytes 256 | tf_op jit(solution)/shard_map/psum | solution.py:95
  433.7 0.9 copy.174
  435.7 1.2 fusion.95
  436.8 3.8 fusion.6
  440.6 3.9 fusion.12
  444.5 3.8 fusion.18
  448.3 4.9 copy_bitcast_fusion
  453.2 3.6 gather_fusion.4
  456.8 2.4 fusion.124
  459.2 2.9 fusion.84
  462.7 1.0 copy-done.4
  463.7 1.6 convolution_bitcast_fusion.3
  465.3 3.2 gather_fusion.5
  468.5 3.1 bitcast_select_fusion
  471.6 4.8 all-to-all-start.3
  476.3 13.9 %psum.47 = f32[]{:T(128)} all-reduce(f32[]{:T(128)} %get-tuple-element.11), channel_id=1, replica_groups=mesh['net'=32,'scen'=8] {'scen'}, use_global_device_ids=true, to_apply=%region_15.18 | all-reduce | flops 1 | bytes 8 | tf_op jit(solution)/shard_map/psum | solution.py:85
  490.9 1.3 fusion.211
  492.3 83.1 %psum.46 = f32[32]{0:T(128)S(1)} all-reduce(f32[32]{0:T(128)S(1)} %broadcast_multiply_fusion), channel_id=1, replica_groups=mesh['net'=32,'scen'=8] {'net'}, use_global_device_ids=true, to_apply=%region_13.16 | all-reduce | flops 32 | bytes 256 | tf_op jit(solution)/shard_map/psum | solution.py:95
  576.0 4.8 convolution_bitcast_fusion
  580.8 3.1 fusion.105
  583.9 2.9 copy.140
  588.0 1.0 fusion.154
  (111 shorter events, 18.1 us)
Async XLA Ops:
  7.2 95.5 %copy-start = (bf16[64,128,128]{2,1,0:T(8,128)(2,1)S(1)}, bf16[64,128,128]{2,1,0:T(8,128)(2,1)}, u32[]{:S(2)}) copy-start(bf16[64,128,128]{2,1,0:T(8,128)(2,1)} %param.23) | copy-start | bytes 6291460
  7.2 87.0 %all-gather.4.cloned.1.call-start = ((), (), s32[]{:S(2)}) async-start(), calls=%async_computation.4 | async-start | bytes 4325376 | tf_op jit(solution)/shard_map/all_gather | solution.py:68
  10.9 105.9 %all-to-all-start = ((s32[32,1,4]{2,1,0:T(1,128)}), s32[32,1,4]{2,1,0:T(1,128)S(1)}, u32[]{:S(2)}, u32[]{:S(2)}) async-start(s32[32,1,4]{2,1,0:T(1,128)} %bitcast.20), calls=%async_computation | async-start | bytes 32768 | tf_op jit(solution)/shard_map/all_to_all | solution.py:54
  102.7 2.4 copy-start.9
  102.7 2.4 copy-start.11
  102.7 2.5 copy-start.22
  105.2 3.0 copy-start.3
  105.2 3.0 copy-start.25
  105.2 3.0 copy-start.27
  108.8 14.9 %copy-start.1 = (f32[32,8192]{1,0:T(8,128)}, f32[32,8192]{1,0:T(8,128)S(1)}, u32[]{:S(2)}) copy-start(f32[32,8192]{1,0:T(8,128)S(1)} %get-tuple-element.21) | copy-start | bytes 3145732
  116.7 53.5 %all-to-all-start.1 = ((f32[32,32,4,128]{3,0,2,1:T(8,128)}), f32[32,32,4,128]{3,0,2,1:T(8,128)}, u32[]{:S(2)}, u32[]{:S(2)}) async-start(f32[32,32,4,128]{3,0,2,1:T(8,128)} %bitcast.330), calls=%async_computation.1 | async-start | bytes 4194304 | tf_op jit(solution)/shard_map/all_to_all | solution.py:105
  122.2 154.5 %all-gather.6.cloned.1.call-start = ((), (), s32[]{:S(2)}) async-start(), calls=%async_computation.5 | async-start | bytes 4325376 | tf_op jit(solution)/shard_map/all_gather | solution.py:68
  125.2 4.9 copy-start.26
  173.2 1.2 copy-start.5
  173.2 1.2 copy-start.16
  173.2 89.2 %copy-start.28 = (f32[32]{0:T(128)S(1)}, f32[32]{0:T(128)}, u32[]{:S(2)}) copy-start(f32[32]{0:T(128)} %param.18) | copy-start | bytes 388
  173.7 0.7 copy-start.13
  285.1 2.4 copy-start.10
  285.1 2.4 copy-start.12
  285.1 2.4 copy-start.23
  287.6 3.0 copy-start.2
  299.1 41.2 %all-to-all-start.2 = ((f32[32,32,4,128]{3,0,2,1:T(8,128)}), f32[32,32,4,128]{3,0,2,1:T(8,128)}, u32[]{:S(2)}, u32[]{:S(2)}) async-start(f32[32,32,4,128]{3,0,2,1:T(8,128)} %bitcast.331), calls=%async_computation.2 | async-start | bytes 4194304 | tf_op jit(solution)/shard_map/all_to_all | solution.py:105
  303.8 144.4 %all-gather.8.cloned.1.call-start = ((), (), s32[]{:S(2)}) async-start(), calls=%async_computation.6 | async-start | bytes 4325376 | tf_op jit(solution)/shard_map/all_gather | solution.py:68
  340.3 3.0 copy-start.24
  343.3 1.2 copy-start.14
  343.3 1.2 copy-start.17
  343.8 0.7 copy-start.19
  456.8 2.4 copy-start.6
  456.8 2.4 copy-start.7
  456.8 2.5 copy-start.8
  456.8 2.5 copy-start.21
  462.7 1.0 copy-start.4
  471.6 112.3 %all-to-all-start.3 = ((f32[32,32,4,128]{3,0,2,1:T(8,128)}), f32[32,32,4,128]{3,0,2,1:T(8,128)}, u32[]{:S(2)}, u32[]{:S(2)}) async-start(f32[32,32,4,128]{3,0,2,1:T(8,128)} %bitcast.329), calls=%async_computation.3 | async-start | bytes 4194304 | tf_op jit(solution)/shard_map/all_to_all | solution.py:105
  586.8 1.0 copy-start.15
  586.8 1.0 copy-start.18
  586.9 1.1 copy-start.20
Sparse Core Ops, SparseCore 0:
  11.2 83.0 all-gather.3
  175.3 78.6 all-gather.5
  345.5 77.5 all-gather.7
where the time goes:
time: 605 us; the launch traced here: 597 us
  blocking collectives  269 us (44%)
  waiting for transfers between devices  122 us (20%)
  matrix products  85.9 us (14%)
  local copies, waits for them, and re-layouts  50.6 us (8%)
  other arithmetic  25.8 us (4%)
  starting transfers between devices  25.4 us (4%)
  between operations  18.3 us (3%)
    psum x3, blocking collectives, per_device(): losses = lax.psum(partial_value, 'net')  229 us
    all_to_all x3, waiting for transfers between devices, per_device(): lax.all_to_all(term_pack.reshape(scen_rows, net_size, slot_cap, block_row...  62.9 us
    all_gather x3, waiting for transfers between devices, per_device(): gathered = lax.all_gather(dual_panel, 'net', axis=1, tiled=True)  58.6 us
    dot_general x12, matrix products, per_device(): jnp.einsum('sjn,jmn->sjm', local_rows, local_blocks[:, touched], preferre...  41.3 us
    psum x3, blocking collectives, per_device(): mean_risk = lax.psum(jnp.sum(risk_now), 'scen') / scen_total  40 us
    all_to_all x3, starting transfers between devices, per_device(): lax.all_to_all(term_pack.reshape(scen_rows, net_size, slot_cap, block_row...  15 us
    reshape x3, local copies, waits for them, and re-layouts, per_device(): gathered.reshape(scen_rows, -1, block_rows)  14.6 us
    dot_general x3, matrix products, per_device(): jnp.einsum('sjm,jkmn->sjkn', flow_grid, local_blocks, preferred_element_t...  14.5 us
  transfers between devices with their start and end apart: 7, of which 3 were waited for; matrix products, arithmetic and copies ran while one was open for 17% of the time, Pallas kernels for 0%

commit v1 on v0

v1 whole, which is shorter than its diff:
```python
import functools

import jax
import jax.numpy as jnp
from jax import lax
from jax.experimental import pallas as pl
from jax.experimental.pallas import tpu as pltpu
from jax.sharding import PartitionSpec as P

ROUNDS = 3
NZ = 8
SLOT = 4
PRIMAL = 0.5
DUAL = 0.5
RISK = 1.0
TAIL = 2.0
MESH = pl.DeviceIdType.MESH
NT = (((1,), (1,)), ((), ()))
F32 = jnp.float32
BF16 = jnp.bfloat16
ORDER = (4, 3, 5, 2, 6, 1, 7, 0)
GROUPS = ((0, 1), (1, 2), (3, 2), (5, 2), (7, 1))


def table_kernel(nx, node_blks, head_ref, index_ref, pos_ref, arc_ref, want_ref, prev_ref, last_ref, count):
    arc_blks, touches = index_ref.shape
    me = lax.axis_index("net")
    x, z = me // NZ, me % NZ
    slots = NZ * SLOT

    def clear(i, _):
        arc_ref[i] = 0
        want_ref[i // slots, i % slots] = node_blks
        return 0

    lax.fori_loop(0, nx * slots, clear, 0)

    def clear_count(i, _):
        count[i] = 0
        return 0

    lax.fori_loop(0, nx * NZ, clear_count, 0)

    def clear_last(b, _):
        last_ref[b] = arc_blks * touches
        return 0

    lax.fori_loop(0, node_blks, clear_last, 0)

    def place(j, _):
        head = head_ref[j]
        dev = head // node_blks
        e = (x - dev // NZ + nx) % nx
        o = (z - dev % NZ + NZ) % NZ
        w = jnp.where(o >= 4, 2 * (o - 4), 7 - 2 * o)
        rank = count[e * NZ + w]
        count[e * NZ + w] = rank + 1
        inside = w * SLOT + rank
        pos_ref[j] = e * slots + inside
        arc_ref[e * slots + inside] = j
        want_ref[e, inside] = head % node_blks
        for k in range(touches):
            b = index_ref[j, k]
            prev_ref[j * touches + k] = last_ref[b]
            last_ref[b] = j * touches + k
        return 0

    lax.fori_loop(0, arc_blks, place, 0)


def main_kernel(
    nx,
    ns,
    scen_total,
    arc_total,
    duals_hbm,
    flows_hbm,
    demand_ref,
    cost_ref,
    excess_in,
    risk_in,
    level_in,
    local_hbm,
    head_hbm,
    index_ref,
    pos_ref,
    arc_ref,
    want_ref,
    want_vec,
    prev_ref,
    last_ref,
    flows_ref,
    duals_ref,
    excess_out,
    risk_out,
    level_out,
    local_ref,
    head_ref,
    c0, c1, c2, c3, c4, c5, c6, c7,
    ask_vec,
    ask_ref,
    chain_prev,
    chain_last,
    pull_ref,
    panel_ref,
    term_ref,
    seg_ref,
    segx_ref,
    x_in,
    x_out,
    fx_in,
    fx_out,
    sl_ref,
    sr_ref,
    ll_ref,
    rr_ref,
    excess_ref,
    risk_ref,
    level_ref,
    lossx,
    lossz,
    scen_rows,
    load_sem,
    ask_send, ask_recv,
    ag_send, ag_recv,
    x_send, x_recv,
    f_send, f_recv,
    r_send, r_recv,
    lx_send, lx_recv,
    lz_send, lz_recv,
    sc_send, sc_recv,
):
    chunks = (c0, c1, c2, c3, c4, c5, c6, c7)
    arc_blks = pos_ref.shape[0]
    touches = local_ref.shape[1]
    rows = panel_ref.shape[1]
    blk = panel_ref.shape[2]
    node_blks = c0.shape[0]
    half = node_blks // 2
    me = lax.axis_index("net")
    scen = lax.axis_index("scen")
    x, z = me // NZ, me % NZ

    def x_peer(e):
        return {"net": lax.rem(x + e, nx) * NZ + z}

    def z_peer(d):
        return {"net": x * NZ + lax.rem(z + d, NZ)}

    def s_peer(d):
        return {"scen": lax.rem(scen + d, ns)}

    def remote(src, dst, send, recv, device):
        return pltpu.make_async_remote_copy(
            src_ref=src, dst_ref=dst, send_sem=send, recv_sem=recv, device_id=device, device_id_type=MESH
        )

    def columns(b):
        return pl.ds(pl.multiple_of(b * blk, blk), blk)

    def ag_copy(direction, step, h):
        n = step if direction == 0 else (NZ - step)
        src = chunks[step - 1] if direction == 0 else chunks[(NZ - step + 1) % NZ]
        part = pl.ds(h * half, half)
        i = direction * 8 + (step - 1) * 2 + h
        return remote(
            src.at[part], chunks[n].at[part], ag_send.at[i], ag_recv.at[i], z_peer(1 if direction == 0 else NZ - 1)
        )

    def x_copy(g, e):
        first, count = GROUPS[g]
        part = pl.ds(first * SLOT, count * SLOT)
        i = g * (nx - 1) + e - 1
        return remote(
            x_out.at[e - 1, part], x_in.at[e, part], x_send.at[i], x_recv.at[i], x_peer(e)
        )

    def f_copy(g, e):
        first, count = GROUPS[g]
        part = pl.ds(first * SLOT, count * SLOT)
        i = g * (nx - 1) + e - 1
        return remote(
            fx_out.at[e - 1, part], fx_in.at[e - 1, part], f_send.at[i], f_recv.at[i], x_peer(nx - e)
        )

    def rs_copy(direction, step, h):
        src = (sl_ref if direction == 0 else sr_ref).at[step - 1]
        dst = (ll_ref if direction == 0 else rr_ref).at[step - 1]
        part = pl.ds(h * half, half)
        i = direction * 8 + (step - 1) * 2 + h
        return remote(
            src.at[part], dst.at[part], r_send.at[i], r_recv.at[i], z_peer(NZ - 1 if direction == 0 else 1)
        )

    def lx_copy(r, e):
        i = r * (nx - 1) + e - 1
        return remote(lossx.at[r, x], lossx.at[r, x], lx_send.at[i], lx_recv.at[i], x_peer(e))

    def lz_copy(r, d):
        i = r * (NZ - 1) + d - 1
        return remote(lossz.at[r, z], lossz.at[r, z], lz_send.at[i], lz_recv.at[i], z_peer(d))

    def sc_copy(r, d):
        i = r * (ns - 1) + d - 1
        return remote(scen_rows.at[r, scen], scen_rows.at[r, scen], sc_send.at[i], sc_recv.at[i], s_peer(d))

    def ask_copy(e):
        return remote(
            want_vec.at[pl.ds(e, 1)], ask_vec.at[pl.ds(e, 1)], ask_send.at[e - 1], ask_recv.at[e - 1], x_peer(nx - e)
        )

    def start_ring():
        for h in range(2):
            ag_copy(0, 1, h).start()
            ag_copy(1, 1, h).start()

    load_duals = pltpu.make_async_copy(duals_hbm, duals_ref, load_sem.at[0])
    load_local = pltpu.make_async_copy(local_hbm, local_ref, load_sem.at[1])
    load_flows = pltpu.make_async_copy(flows_hbm, flows_ref, load_sem.at[2])
    load_heads = pltpu.make_async_copy(head_hbm, head_ref, load_sem.at[3])
    load_duals.start()
    load_local.start()
    load_flows.start()
    load_heads.start()
    barrier = pltpu.get_barrier_semaphore()
    peers = (
        [x_peer(e) for e in range(1, nx)] + [z_peer(d) for d in range(1, NZ)] + [s_peer(d) for d in range(1, ns)]
    )
    for peer in peers:
        pl.semaphore_signal(barrier, inc=1, device_id=peer, device_id_type=MESH)
    lane = lax.broadcasted_iota(jnp.int32, (rows, blk), 1)
    diagonal = lax.broadcasted_iota(jnp.int32, (rows, blk), 0) == lane
    real = lax.broadcasted_iota(jnp.int32, (1, blk), 1) < rows
    excess_ref[...] = jnp.zeros_like(excess_ref)
    risk_ref[...] = jnp.zeros_like(risk_ref)
    excess_ref[:, 0:rows] = excess_in[...]
    risk_ref[:, 0:rows] = risk_in[...]
    level_ref[...] = jnp.broadcast_to(level_in[...], level_ref.shape)
    seg_ref[arc_blks * touches] = jnp.zeros((rows, blk), F32)
    segx_ref[0] = jnp.zeros((rows, blk), F32)
    load_duals.wait()
    for b in range(node_blks):
        c0[b] = duals_ref[:, b * blk : (b + 1) * blk].astype(BF16)
    pl.semaphore_wait(barrier, len(peers))
    for e in range(1, nx):
        ask_copy(e).start()
    start_ring()

    for e in range(1, nx):
        ask_copy(e).wait_recv()
    to_scalar = pltpu.make_async_copy(ask_vec, ask_ref, load_sem.at[4])
    to_scalar.start()
    to_scalar.wait()
    for e in range(1, nx):
        ask_copy(e).wait_send()

    def asked(e, s):
        return want_ref[0, s] if e == 0 else ask_ref[e, s]

    def chain_tables(w, _):
        named = [asked(q // SLOT, w * SLOT + q % SLOT) for q in range(nx * SLOT)]
        for q in range(nx * SLOT):
            found = jnp.int32(0)
            for p in range(q):
                found = jnp.where(named[p] == named[q], w * (nx * SLOT) + p + 1, found)
            chain_prev[w * (nx * SLOT) + q] = found
        for b in range(node_blks):
            found = jnp.int32(0)
            for q in range(nx * SLOT):
                found = jnp.where(named[q] == b, w * (nx * SLOT) + q + 1, found)
            chain_last[w * node_blks + b] = found
        return 0

    lax.fori_loop(0, NZ, chain_tables, 0)
    load_local.wait()
    load_flows.wait()
    load_heads.wait()

    def pull_local(first, count):
        def body(i, _):
            j = first + i
            total = jnp.zeros((rows, blk), F32)
            for k in range(touches):
                total += lax.dot_general(
                    c0[index_ref[j, k]], local_ref[j, k], NT, preferred_element_type=F32
                )
            pull_ref[j] = total
            return 0

        lax.fori_loop(0, count, body, 0, unroll=4)

    def push_local(first, count):
        def body(i, _):
            j = first + i
            v = panel_ref[j]
            for k in range(touches):
                p = j * touches + k
                term = jnp.dot(v, local_ref[j, k], preferred_element_type=F32)
                seg_ref[p] = term + seg_ref[prev_ref[p]]
            return 0

        lax.fori_loop(0, count, body, 0, unroll=4)

    def answer(w):
        chunk = chunks[ORDER[w]]
        for e in range(nx):
            for s in range(SLOT):
                i = w * SLOT + s
                block = chunk[jnp.minimum(asked(e, i), node_blks - 1)]
                if e == 0:
                    x_in[0, i] = block
                else:
                    x_out[e - 1, i] = block

    def answer_group(g):
        first, count = GROUPS[g]
        for w in range(first, first + count):
            answer(w)
        for e in range(1, nx):
            x_copy(g, e).start()

    def collect(w):
        for q in range(nx * SLOT):
            e, i = q // SLOT, w * SLOT + q % SLOT
            value = term_ref[arc_ref[i]] if e == 0 else fx_in[e - 1, i]
            n = w * (nx * SLOT) + q
            segx_ref[n + 1] = value.astype(F32) + segx_ref[chain_prev[n]]

    def send_sum(direction, step, h, with_arrived):
        w = ORDER.index(5 - step if direction == 0 else 3 + step)
        dst = sl_ref if direction == 0 else sr_ref
        arrived = ll_ref if direction == 0 else rr_ref
        if with_arrived:
            rs_copy(direction, step - 1, h).wait_recv()
        for b in range(h * half, (h + 1) * half):
            value = segx_ref[chain_last[w * node_blks + b]]
            if with_arrived:
                value = value + arrived[step - 2, b].astype(F32)
            dst[step - 1, b] = value.astype(BF16)
        rs_copy(direction, step, h).start()

    def one_round(r, _):
        scen_rows[r, scen] = risk_ref[...]
        for d in range(1, ns):
            sc_copy(r, d).start()
        piece = arc_blks // 8
        answer_group(4)
        pull_local(0, 2 * piece)
        done = 2
        for step in range(1, 4):
            for h in range(2):
                ag_copy(0, step, h).wait_recv()
                if step < 3 or h == 0:
                    ag_copy(0, step + 1, h).start()
                ag_copy(1, step, h).wait_recv()
                if step < 3 or h == 1:
                    ag_copy(1, step + 1, h).start()
                if h == 1:
                    answer_group(4 - step)
                pull_local(done * piece, piece)
                done += 1
        ag_copy(0, 4, 0).wait_recv()
        ag_copy(1, 4, 1).wait_recv()
        answer_group(0)
        risk_wide = jnp.broadcast_to(
            jnp.sum(jnp.where(diagonal, jnp.broadcast_to(risk_ref[...], (rows, blk)), 0.0), axis=1, keepdims=True),
            (rows, blk),
        )
        for g in range(len(GROUPS)):
            for e in range(1, nx):
                x_copy(4 - g, e).wait_recv()

        def head(j, loss):
            pulled = pull_ref[j] + lax.dot_general(
                x_in[pos_ref[j] // (NZ * SLOT), pos_ref[j] % (NZ * SLOT)],
                head_ref[j],
                NT,
                preferred_element_type=F32,
            )
            cost = jnp.broadcast_to(cost_ref[pl.ds(j, 1), :], (rows, blk))
            now = flows_ref[:, columns(j)]
            new = jnp.maximum(now - PRIMAL * (risk_wide * cost - pulled), 0.0)
            bar = 2.0 * new - now
            flows_ref[:, columns(j)] = new
            panel = bar.astype(BF16)
            panel_ref[j] = panel
            term_ref[j] = jnp.dot(panel, head_ref[j], preferred_element_type=F32).astype(BF16)
            return loss + cost * bar

        loss = lax.fori_loop(0, arc_blks, head, jnp.zeros((rows, blk), F32), unroll=4)

        for g, (first, count) in enumerate(GROUPS):
            for e in range(1, nx):
                for i in range(first * SLOT, (first + count) * SLOT):
                    fx_out[e - 1, i] = term_ref[arc_ref[e * NZ * SLOT + i]]
                f_copy(g, e).start()
        wide = jnp.broadcast_to(jnp.sum(loss, axis=1, keepdims=True), (rows, blk))
        lossx[r, x] = jnp.sum(jnp.where(diagonal, wide, 0.0), axis=0, keepdims=True)
        for e in range(1, nx):
            lx_copy(r, e).start()
        for direction in range(2):
            for step in range(1, 5):
                for h in range(2):
                    if step < 4 or h == direction:
                        ag_copy(direction, step, h).wait_send()
        for g in range(len(GROUPS)):
            for e in range(1, nx):
                x_copy(g, e).wait_send()
        push_local(0, 2 * piece)

        for e in range(1, nx):
            f_copy(0, e).wait_recv()
        collect(0)
        send_sum(0, 1, 0, False)
        send_sum(1, 1, 1, False)
        for e in range(1, nx):
            lx_copy(r, e).wait_recv()
        total = lossx[r, 0]
        for i in range(1, nx):
            total = total + lossx[r, i]
        lossz[r, z] = total
        for d in range(1, NZ):
            lz_copy(r, d).start()
        done = 2
        for step in range(2, 5):
            for e in range(1, nx):
                f_copy(step - 1, e).wait_recv()
            collect(2 * step - 3)
            collect(2 * step - 2)
            for turn in range(2):
                send_sum(0, step, 1 - turn, step > 2 or turn == 1)
                send_sum(1, step, turn, step > 2 or turn == 1)
                push_local(done * piece, piece)
                done += 1
        for e in range(1, nx):
            f_copy(4, e).wait_recv()
        collect(7)

        for d in range(1, NZ):
            lz_copy(r, d).wait_recv()
        losses = lossz[r, 0]
        for i in range(1, NZ):
            losses = losses + lossz[r, i]
        losses = losses / arc_total
        for d in range(1, ns):
            sc_copy(r, d).wait_recv()
        risk_sum = scen_rows[r, 0]
        for i in range(1, ns):
            risk_sum = risk_sum + scen_rows[r, i]
        mean = jnp.broadcast_to(jnp.sum(risk_sum, axis=1, keepdims=True), (1, blk)) / scen_total
        risk = risk_ref[...]
        excess = excess_ref[...]
        level = level_ref[...]
        excess_new = jnp.maximum(excess - PRIMAL * (TAIL - risk), 0.0)
        level_new = level - PRIMAL * (1.0 - mean)
        excess_bar = 2.0 * excess_new - excess
        level_bar = 2.0 * level_new - level
        risk_new = jnp.maximum(risk + RISK * (losses - excess_bar - level_bar), 0.0)
        excess_ref[...] = excess_new
        level_ref[...] = level_new
        for d in range(1, ns):
            sc_copy(r, d).wait_send()
        for d in range(1, NZ):
            lz_copy(r, d).wait_send()
        for e in range(1, nx):
            lx_copy(r, e).wait_send()
        risk_ref[...] = jnp.where(real, risk_new, 0.0)

        for turn in range(2):
            rs_copy(0, 4, 1 - turn).wait_recv()
            rs_copy(1, 4, turn).wait_recv()
        for b in range(node_blks):
            pushed = (
                seg_ref[last_ref[b]]
                + segx_ref[chain_last[7 * node_blks + b]]
                + (ll_ref[3, b].astype(F32) + rr_ref[3, b].astype(F32))
            )
            dual = duals_ref[:, b * blk : (b + 1) * blk] + DUAL * (demand_ref[:, b * blk : (b + 1) * blk] - pushed)
            duals_ref[:, b * blk : (b + 1) * blk] = dual
            c0[b] = dual.astype(BF16)
        for direction in range(2):
            for step in range(1, 5):
                for h in range(2):
                    if step > 1 or h == direction:
                        rs_copy(direction, step, h).wait_send()
        for g in range(len(GROUPS)):
            for e in range(1, nx):
                f_copy(g, e).wait_send()

        @pl.when(r < ROUNDS - 1)
        def _():
            start_ring()

        return 0

    lax.fori_loop(0, ROUNDS, one_round, 0)
    excess_out[...] = excess_ref[:, 0:rows]
    risk_out[...] = risk_ref[:, 0:rows]
    level_out[...] = level_ref[:, 0:1]


def per_device(
    arc_flows,
    node_duals,
    demand,
    excess,
    risk_duals,
    threshold,
    arc_costs,
    local_blocks,
    head_blocks,
    local_index,
    head_index,
):
    blk = local_blocks.shape[-1]
    rows, arcs = arc_flows.shape
    arc_blks, touches = local_index.shape
    node_blks = node_duals.shape[1] // blk
    net = lax.axis_size("net")
    ns = lax.axis_size("scen")
    nx = net // NZ
    slots = NZ * SLOT
    smem = pl.BlockSpec(memory_space=pltpu.SMEM)
    vmem = pl.BlockSpec(memory_space=pltpu.VMEM)
    hbm = pl.BlockSpec(memory_space=pl.ANY)

    def ints(*shape):
        return jax.ShapeDtypeStruct(shape, jnp.int32)

    pos, slot_arc, want, prev, last = pl.pallas_call(
        functools.partial(table_kernel, nx, node_blks),
        out_shape=(ints(arc_blks), ints(nx * slots), ints(nx, 128), ints(arc_blks * touches), ints(node_blks)),
        in_specs=[smem, smem],
        out_specs=(smem,) * 5,
        scratch_shapes=[pltpu.SMEM((nx * NZ,), jnp.int32)],
        name="tables",
    )(head_index, local_index)

    def floats(*shape):
        return jax.ShapeDtypeStruct(shape, F32)

    def panel(*lead):
        return pltpu.VMEM((*lead, rows, blk), BF16)

    def wide(*lead):
        return pltpu.VMEM((*lead, rows, blk), F32)

    def row(*lead):
        return pltpu.VMEM((*lead, 1, blk), F32)

    dma = pltpu.SemaphoreType.DMA
    groups = len(GROUPS)
    scratch = (
        [pltpu.VMEM(local_blocks.shape, BF16), pltpu.VMEM(head_blocks.shape, BF16)]
        + [panel(node_blks)] * NZ
        + [
            pltpu.VMEM((nx, 128), jnp.int32),
            pltpu.SMEM((nx, 128), jnp.int32),
            pltpu.SMEM((NZ * nx * SLOT,), jnp.int32),
            pltpu.SMEM((NZ * node_blks,), jnp.int32),
            wide(arc_blks),
            panel(arc_blks),
            panel(arc_blks),
            wide(arc_blks * touches + 1),
            wide(NZ * nx * SLOT + 1),
            panel(nx, slots),
            panel(nx - 1, slots),
            panel(nx - 1, slots),
            panel(nx - 1, slots),
            panel(4, node_blks),
            panel(4, node_blks),
            panel(4, node_blks),
            panel(4, node_blks),
            row(),
            row(),
            row(),
            row(ROUNDS, nx),
            row(ROUNDS, NZ),
            row(ROUNDS, ns),
            dma((5,)),
        ]
        + [dma((nx - 1,))] * 2
        + [dma((16,))] * 2
        + [dma((groups * (nx - 1),))] * 4
        + [dma((16,))] * 2
        + [dma((ROUNDS * (nx - 1),))] * 2
        + [dma((ROUNDS * (NZ - 1),))] * 2
        + [dma((ROUNDS * (ns - 1),))] * 2
    )
    flows, duals, excess, risk, level = pl.pallas_call(
        functools.partial(main_kernel, nx, ns, float(rows * ns), float(arcs * net)),
        out_shape=(floats(rows, arcs), floats(*node_duals.shape), floats(1, rows), floats(1, rows), floats(1, 1)),
        in_specs=[hbm, hbm, vmem, vmem, vmem, vmem, vmem, hbm, hbm, smem, smem, smem, smem, vmem, smem, smem],
        out_specs=(vmem,) * 5,
        scratch_shapes=scratch,
        compiler_params=pltpu.CompilerParams(
            collective_id=0, has_side_effects=True, vmem_limit_bytes=48 * 1024 * 1024
        ),
        name="rounds",
    )(
        node_duals,
        arc_flows,
        demand,
        arc_costs.reshape(arc_blks, blk),
        excess.reshape(1, rows),
        risk_duals.reshape(1, rows),
        threshold.reshape(1, 1),
        local_blocks,
        head_blocks,
        local_index,
        pos,
        slot_arc,
        want,
        want,
        prev,
        last,
    )
    return flows, duals, excess.reshape(-1), risk.reshape(-1), level.reshape(-1)


def solution(mesh):
    placed = (
        P("scen", "net"),
        P("scen", "net"),
        P("scen", "net"),
        P("scen"),
        P("scen"),
        P(),
        P("net"),
        P("net", None, None, None),
        P("net", None, None),
        P("net", None),
        P("net"),
    )
    return jax.shard_map(
        per_device,
        mesh=mesh,
        in_specs=placed,
        out_specs=(P("scen", "net"), P("scen", "net"), P("scen"), P("scen"), P()),
        check_vma=False,
    )
```

time: 605 us -> 208 us (0.34)
  blocking collectives: 269 us -> 0 us
  Pallas kernels: 0 us -> 187 us
  waiting for transfers between devices: 122 us -> 0 us
  matrix products: 85.9 us -> 0 us
  local copies, waits for them, and re-layouts: 50.6 us -> 14.9 us
  other arithmetic: 25.8 us -> 0 us
  starting transfers between devices: 25.4 us -> 0 us
  between operations: 18.3 us -> 3.08 us
    psum x6 -> x0, blocking collectives: 269 us -> none  [the longest x3 229 us: per_device(): losses = lax.psum(partial_value, 'net')]
    pallas_call x0 -> x2, Pallas kernels: none -> 187 us  [the longest x1 181 us: per_device(): pl.pallas_call(functools.partial(main_kernel, nx, ns, float(rows * ns), f...]
    dot_general x39 -> x0, matrix products: 85.9 us -> none  [the longest x12 41.3 us: per_device(): jnp.einsum('sjn,jmn->sjm', local_rows, local_blocks[:, touched], preferre...]
    all_to_all x4 -> x0, waiting for transfers between devices: 62.9 us -> none  [the longest x3 62.9 us: per_device(): lax.all_to_all(term_pack.reshape(scen_rows, net_size, slot_cap, block_row...]
    all_gather x3 -> x0, waiting for transfers between devices: 58.6 us -> none  [per_device(): gathered = lax.all_gather(dual_panel, 'net', axis=1, tiled=True)]
    all_to_all x4 -> x0, starting transfers between devices: 24.6 us -> none  [the longest x3 15 us: per_device(): lax.all_to_all(term_pack.reshape(scen_rows, net_size, slot_cap, block_row...]
    gather x6 -> x0, local copies, waits for them, and re-layouts: 20.4 us -> none  [the longest x3 10.8 us: per_device(): jnp.take(gathered.reshape(scen_rows, -1, block_rows), head_index, axis=1)]
    reshape x3 -> x0, local copies, waits for them, and re-layouts: 14.6 us -> none  [per_device(): gathered.reshape(scen_rows, -1, block_rows)]
  transfers between devices with their start and end apart: 7 -> 0, of which waited for: 3 -> 0; matrix products, arithmetic and copies ran while one was open for 17% -> 0% of each run, Pallas kernels for 0% -> 0%
where the time goes in v1:
time: 208 us; the launch traced here: 205 us
  Pallas kernels  187 us (90%)
  local copies, waits for them, and re-layouts  14.9 us (7%)
  between operations  3.08 us (1%)
    pallas_call x1, Pallas kernels, per_device(): pl.pallas_call(functools.partial(main_kernel, nx, ns, float(rows * ns), f...  181 us
    unnamed x31, local copies, waits for them, and re-layouts  14.9 us
    pallas_call x1, Pallas kernels, per_device(): pl.pallas_call(functools.partial(table_kernel, nx, node_blks), out_shape=...  6.11 us

profile of v1, /device:TPU:0, one launch (start us, length us, event | category | flops | bytes accessed | tf_op | source)
XLA Modules:
  0.0 205.1 jit_solution(5185943552477116677)
XLA Ops:
  1.3 1.4 copy.17.index_ref
  2.7 6.1 %tables.1 = (s32[64]{0:T(128)}, s32[128]{0:T(128)}, s32[4,128]{1,0:T(4,128)}, s32[256]{0:T(256)}, s32[16]{0:T(128)}) custom-call(s32[64]{0:T(128)} %head_ref.1, s32[64,4]{1,0:T(8,128)} %copy.17.index_ref), custom_call_target="tpu_custom_call" | custom-call | tf_op jit(solution)/shard_map/tables/pallas_call | solution.py:530
  8.8 0.0 copy-start
  8.8 1.6 copy-done
  10.4 0.0 copy-start.1
  10.4 1.2 copy-done.1
  11.6 0.0 copy-start.2
  11.6 0.8 copy-done.2
  12.4 0.0 copy-start.3
  12.4 0.9 copy-done.3
  13.3 0.0 copy-start.4
  13.3 0.9 copy-done.4
  14.3 0.0 copy-start.5
  14.3 0.8 copy-done.5
  15.0 0.0 copy-start.6
  15.0 0.7 copy-done.6
  15.7 0.0 copy-start.7
  15.7 0.6 copy-done.7
  16.3 0.0 copy-start.8
  16.3 0.7 copy-done.8
  17.0 0.0 copy-start.9
  17.0 0.7 copy-done.9
  17.6 0.0 copy-start.10
  17.6 0.7 copy-done.10
  18.3 0.0 copy-start.11
  18.3 0.7 copy-done.11
  19.0 0.0 copy-start.12
  19.0 0.7 copy-done.12
  19.6 181.0 %rounds.1 = (f32[32,8192]{1,0:T(8,128)S(1)}, f32[32,2048]{1,0:T(8,128)S(1)}, f32[1,32]{1,0:T(1,128)S(1)}, f32[1,32]{1,0:T(1,128)S(1)}, f32[1,1]{1,0:T(1,128)}) custom-call(f32[32,2048]{1,0:T(8,128)S(1)} %copy-done.3, f32[32,8192]{1,0:T(8,128)S(1)} %copy-done.1, f32[32,2048]{1,0:T(8,128)S(1)} %copy-done.4, f32[64,128]{1,0:T(8,128)S(1)} %bitcast.8, ...), custom_call_target="tpu_custom_call" | custom-call | tf_op jit(solution)/shard_map/rounds/pallas_call | solution.py:590
  200.6 1.0 copy.24
  201.6 0.7 copy.25
  202.3 0.5 copy.26
  202.8 0.5 copy.27
Async XLA Ops:
  8.8 1.6 copy-start
  10.4 1.2 copy-start.1
  11.6 0.8 copy-start.2
  12.4 0.9 copy-start.3
  13.3 0.9 copy-start.4
  14.3 0.8 copy-start.5
  15.0 0.7 copy-start.6
  15.7 0.6 copy-start.7
  16.3 0.7 copy-start.8
  17.0 0.7 copy-start.9
  17.6 0.7 copy-start.10
  18.3 0.7 copy-start.11
  19.0 0.7 copy-start.12

commit v2 on v1

v2 whole, which is shorter than its diff:
```python
import functools

import jax
import jax.numpy as jnp
from jax import lax
from jax.experimental import pallas as pl
from jax.experimental.pallas import tpu as pltpu
from jax.sharding import PartitionSpec as P

ROUNDS = 3
NZ = 8
SLOT = 4
PRIMAL = 0.5
DUAL = 0.5
RISK = 1.0
TAIL = 2.0
MESH = pl.DeviceIdType.MESH
NT = (((1,), (1,)), ((), ()))
F32 = jnp.float32
BF16 = jnp.bfloat16
ORDER = (4, 3, 5, 2, 6, 1, 7, 0)
GROUPS = ((0, 1), (1, 2), (3, 2), (5, 2), (7, 1))
PARTS = 4
TURNS = ((0, 1, 2, 3), (2, 3, 0, 1))


def halves(n):
    return n.bit_length() - 1


def table_kernel(nx, node_blks, owner_vec, index_vec, own_rows, want_vec):
    touches, arc_blks = index_vec.shape
    blk = own_rows.shape[1]
    slots = NZ * SLOT
    me = lax.axis_index("net")
    x, z = me // NZ, me % NZ

    def count_of(mask, axis):
        return jnp.sum(jnp.where(mask, 1.0, 0.0), axis=axis, keepdims=True).astype(jnp.int32)

    def upright(row):
        n = row.shape[1]
        eye = lax.broadcasted_iota(jnp.int32, (n, n), 0) == lax.broadcasted_iota(jnp.int32, (n, n), 1)
        wide = jnp.broadcast_to(row.astype(F32), (n, n))
        return jnp.sum(jnp.where(eye, wide, 0.0), axis=1, keepdims=True).astype(jnp.int32)

    def highest(mask, value):
        return jnp.max(jnp.where(mask, value, 0.0), axis=0, keepdims=True)

    def place(heads):
        dev = lax.shift_right_logical(heads, halves(node_blks))
        e = (x - lax.shift_right_logical(dev, halves(NZ)) + nx) & (nx - 1)
        o = (z - (dev & (NZ - 1)) + NZ) & (NZ - 1)
        w = jnp.where(o >= 4, 2 * (o - 4), 7 - 2 * o)
        return dev, e * slots + w * SLOT

    square = (arc_blks, arc_blks)
    upper = lax.broadcasted_iota(jnp.int32, square, 0) < lax.broadcasted_iota(jnp.int32, square, 1)
    lower = lax.broadcasted_iota(jnp.int32, square, 0) > lax.broadcasted_iota(jnp.int32, square, 1)
    equal = lax.broadcasted_iota(jnp.int32, square, 0) == lax.broadcasted_iota(jnp.int32, square, 1)
    heads = owner_vec[...]
    heads_up = upright(heads)
    dev, base = place(heads)
    dev_up, base_up = place(heads_up)
    same = dev_up == dev
    pos = base + jnp.minimum(count_of(same & upper, 0), SLOT - 1)
    pos_up = base_up + jnp.minimum(count_of(same & lower, 1), SLOT - 1)
    flat = (arc_blks, nx * slots)
    filled = pos_up == lax.broadcasted_iota(jnp.int32, flat, 1)
    arc_number = lax.broadcasted_iota(jnp.int32, flat, 0).astype(F32)
    inside_up = (heads_up & (node_blks - 1)).astype(F32)
    arcs = highest(filled, arc_number)
    want = node_blks - highest(filled, node_blks - inside_up).astype(jnp.int32)
    want_vec[...] = want
    own_rows[...] = jnp.zeros_like(own_rows)
    own_rows[0:1, 0:arc_blks] = pos
    own_rows[1:2, :] = arcs.astype(jnp.int32)
    own_rows[7:8, :] = want
    step_up = lax.broadcasted_iota(jnp.int32, square, 0).astype(F32) * touches
    column = [upright(index_vec[k : k + 1, :]) for k in range(touches)]
    final = jnp.zeros((1, blk), F32)
    for k in range(touches):
        row = index_vec[k : k + 1, :]
        found = jnp.zeros((1, arc_blks), F32)
        for q in range(touches):
            before = (upper | equal) if q < k else upper
            found = jnp.maximum(found, highest((column[q] == row) & before, step_up + (q + 1)))
        own_rows[2 + k : 3 + k, 0:arc_blks] = found.astype(jnp.int32)
        wide = (arc_blks, blk)
        named = column[k] == lax.broadcasted_iota(jnp.int32, wide, 1)
        final = jnp.maximum(
            final, highest(named, lax.broadcasted_iota(jnp.int32, wide, 0).astype(F32) * touches + (k + 1))
        )
    own_rows[2 + touches : 3 + touches, :] = final.astype(jnp.int32)


def main_kernel(
    nx,
    ns,
    scen_total,
    arc_total,
    duals_hbm,
    flows_hbm,
    demand_hbm,
    cost_ref,
    excess_in,
    risk_in,
    level_in,
    local_hbm,
    head_hbm,
    index_ref,
    own_tab,
    want_vec,
    flows_out,
    duals_ref,
    excess_out,
    risk_out,
    level_out,
    local_ref,
    head_ref,
    flows_ref,
    demand_ref,
    c0, c1, c2, c3, c4, c5, c6, c7,
    ask_vec,
    ask_ref,
    ask_tab,
    pull_ref,
    panel_ref,
    seg_ref,
    segx_ref,
    hp_ref,
    own_ref,
    x_in,
    x_out,
    fx_in,
    fx_out,
    sl_ref,
    sr_ref,
    ll_ref,
    rr_ref,
    excess_ref,
    risk_ref,
    level_ref,
    lossx,
    lossz,
    scen_rows,
    load_sem,
    ask_send, ask_recv,
    ag_send, ag_recv,
    x_send, x_recv,
    f_send, f_recv,
    r_send, r_recv,
    lx_send, lx_recv,
    lz_send, lz_recv,
    sc_send, sc_recv,
):
    chunks = (c0, c1, c2, c3, c4, c5, c6, c7)
    touches, arc_blks = index_ref.shape
    rows = panel_ref.shape[1]
    blk = panel_ref.shape[2]
    node_blks = c0.shape[0]
    part_blks = node_blks // PARTS
    slots = NZ * SLOT
    me = lax.axis_index("net")
    scen = lax.axis_index("scen")
    x, z = me // NZ, me % NZ

    def x_peer(e):
        return {"net": lax.rem(x + e, nx) * NZ + z}

    def z_peer(d):
        return {"net": x * NZ + lax.rem(z + d, NZ)}

    def s_peer(d):
        return {"scen": lax.rem(scen + d, ns)}

    def remote(src, dst, send, recv, device):
        return pltpu.make_async_remote_copy(
            src_ref=src, dst_ref=dst, send_sem=send, recv_sem=recv, device_id=device, device_id_type=MESH
        )

    def columns(b):
        return pl.ds(pl.multiple_of(b * blk, blk), blk)

    def part(h):
        return pl.ds(h * part_blks, part_blks)

    def ag_copy(direction, step, h):
        n = step if direction == 0 else (NZ - step)
        src = chunks[step - 1] if direction == 0 else chunks[(NZ - step + 1) % NZ]
        i = (direction * 4 + step - 1) * PARTS + h
        return remote(
            src.at[part(h)], chunks[n].at[part(h)], ag_send.at[i], ag_recv.at[i], z_peer(1 if direction == 0 else NZ - 1)
        )

    def x_copy(g, e):
        first, count = GROUPS[g]
        i = g * (nx - 1) + e - 1
        return remote(
            x_out.at[pl.ds(e * slots + first * SLOT, count * SLOT)],
            x_in.at[pl.ds(e * slots + first * SLOT, count * SLOT)],
            x_send.at[i], x_recv.at[i], x_peer(e),
        )

    def f_copy(g, e):
        first, count = GROUPS[g]
        i = g * (nx - 1) + e - 1
        return remote(
            fx_out.at[pl.ds(e * slots + first * SLOT, count * SLOT)],
            fx_in.at[pl.ds(e * slots + first * SLOT, count * SLOT)],
            f_send.at[i], f_recv.at[i], x_peer(nx - e),
        )

    def rs_copy(direction, step, h):
        src = (sl_ref if direction == 0 else sr_ref).at[step - 1]
        dst = (ll_ref if direction == 0 else rr_ref).at[step - 1]
        i = (direction * 4 + step - 1) * PARTS + h
        return remote(
            src.at[part(h)], dst.at[part(h)], r_send.at[i], r_recv.at[i], z_peer(NZ - 1 if direction == 0 else 1)
        )

    def lx_copy(r, e):
        i = r * (nx - 1) + e - 1
        return remote(lossx.at[r, x], lossx.at[r, x], lx_send.at[i], lx_recv.at[i], x_peer(e))

    def lz_copy(r, d):
        i = r * (NZ - 1) + d - 1
        return remote(lossz.at[r, z], lossz.at[r, z], lz_send.at[i], lz_recv.at[i], z_peer(d))

    def sc_copy(r, d):
        i = r * (ns - 1) + d - 1
        return remote(scen_rows.at[r, scen], scen_rows.at[r, scen], sc_send.at[i], sc_recv.at[i], s_peer(d))

    def ask_copy(e):
        return remote(want_vec, ask_vec.at[pl.ds(e, 1)], ask_send.at[e - 1], ask_recv.at[e - 1], x_peer(nx - e))

    def start_ring():
        for turn in range(PARTS):
            ag_copy(0, 1, TURNS[0][turn]).start()
            ag_copy(1, 1, TURNS[1][turn]).start()

    loads = [
        pltpu.make_async_copy(src, dst, load_sem.at[i])
        for i, (src, dst) in enumerate(
            (
                (duals_hbm, duals_ref),
                (local_hbm, local_ref),
                (head_hbm, head_ref),
                (flows_hbm, flows_ref),
                (demand_hbm, demand_ref),
            )
        )
    ]
    for load in loads:
        load.start()
    barrier = pltpu.get_barrier_semaphore()
    peers = (
        [x_peer(e) for e in range(1, nx)] + [z_peer(d) for d in range(1, NZ)] + [s_peer(d) for d in range(1, ns)]
    )
    for peer in peers:
        pl.semaphore_signal(barrier, inc=1, device_id=peer, device_id_type=MESH)
    lane = lax.broadcasted_iota(jnp.int32, (rows, blk), 1)
    diagonal = lax.broadcasted_iota(jnp.int32, (rows, blk), 0) == lane
    real = lax.broadcasted_iota(jnp.int32, (1, blk), 1) < rows
    excess_ref[...] = jnp.zeros_like(excess_ref)
    risk_ref[...] = jnp.zeros_like(risk_ref)
    excess_ref[:, 0:rows] = excess_in[...]
    risk_ref[:, 0:rows] = risk_in[...]
    level_ref[...] = jnp.broadcast_to(level_in[...], level_ref.shape)
    seg_ref[0] = jnp.zeros((rows, blk), F32)
    segx_ref[0] = jnp.zeros((rows, blk), F32)

    loads[0].wait()
    for b in range(node_blks):
        c0[b] = duals_ref[:, b * blk : (b + 1) * blk].astype(BF16)
    pl.semaphore_wait(barrier, len(peers))
    for e in range(1, nx):
        ask_copy(e).start()
    start_ring()

    for e in range(1, nx):
        ask_copy(e).wait_recv()
    to_scalar = pltpu.make_async_copy(ask_vec, ask_ref, load_sem.at[5])
    to_scalar.start()
    to_scalar.wait()
    for e in range(1, nx):
        ask_copy(e).wait_send()

    def chain_tables(w, _):
        places = [q // SLOT * slots + w * SLOT + q % SLOT for q in range(nx * SLOT)]
        named = [
            own_tab[touches + 3, i] if q < SLOT else ask_ref[q // SLOT, i] for q, i in enumerate(places)
        ]
        for q, i in enumerate(places):
            found = jnp.int32(0)
            for p in range(q):
                found = jnp.where(named[p] == named[q], places[p] + 1, found)
            ask_tab[0, i] = jnp.minimum(named[q], node_blks - 1)
            ask_tab[1, i] = found
        for b in range(node_blks):
            found = jnp.int32(0)
            for q, i in enumerate(places):
                found = jnp.where(named[q] == b, i + 1, found)
            ask_tab[2, w * node_blks + b] = found
        return 0

    lax.fori_loop(0, NZ, chain_tables, 0)
    for load in loads[1:]:
        load.wait()

    def pull_local(first, count):
        def body(i, _):
            j = first + i
            total = jnp.zeros((rows, blk), F32)
            for k in range(touches):
                total += lax.dot_general(
                    c0[index_ref[k, j]], local_ref[j, k], NT, preferred_element_type=F32
                )
            pull_ref[j] = total
            return 0

        lax.fori_loop(0, count, body, 0, unroll=4)

    def push_local(first, count):
        def body(i, _):
            j = first + i
            v = panel_ref[j]
            for k in range(touches):
                term = jnp.dot(v, local_ref[j, k], preferred_element_type=F32)
                seg_ref[j * touches + k + 1] = term + seg_ref[own_tab[2 + k, j]]
            return 0

        lax.fori_loop(0, count, body, 0, unroll=4)

    def answer_group(g):
        first, count = GROUPS[g]
        for e in range(nx):
            for w in range(first, first + count):
                chunk = chunks[ORDER[w]]
                for s in range(SLOT):
                    i = e * slots + w * SLOT + s
                    (x_in if e == 0 else x_out)[i] = chunk[ask_tab[0, i]]
            if e > 0:
                x_copy(g, e).start()

    def pull_heads(g):
        first, count = GROUPS[g]

        def body(e, _):
            for s in range(count * SLOT):
                i = e * slots + first * SLOT + s
                hp_ref[i] = lax.dot_general(x_in[i], head_ref[own_tab[1, i]], NT, preferred_element_type=F32)
            return 0

        for e in range(1, nx):
            x_copy(g, e).wait_recv()
        lax.fori_loop(0, nx, body, 0)

    def push_heads(g):
        first, count = GROUPS[g]

        def term(e, s):
            j = own_tab[1, e * slots + first * SLOT + s]
            return jnp.dot(panel_ref[j], head_ref[j], preferred_element_type=F32)

        def body(e, _):
            for s in range(count * SLOT):
                fx_out[e * slots + first * SLOT + s] = term(e, s).astype(BF16)
            return 0

        lax.fori_loop(1, nx, body, 0)
        for e in range(1, nx):
            f_copy(g, e).start()
        for s in range(count * SLOT):
            own_ref[first * SLOT + s] = term(0, s)

    def collect(w):
        for q in range(nx * SLOT):
            e = q // SLOT
            i = w * SLOT + q % SLOT
            n = e * slots + i
            value = own_ref[i] if e == 0 else fx_in[n].astype(F32)
            segx_ref[n + 1] = value + segx_ref[ask_tab[1, n]]

    def send_sum(direction, step, h, with_arrived):
        w = ORDER.index(5 - step if direction == 0 else 3 + step)
        dst = sl_ref if direction == 0 else sr_ref
        arrived = ll_ref if direction == 0 else rr_ref
        if with_arrived:
            rs_copy(direction, step - 1, h).wait_recv()
        for b in range(h * part_blks, (h + 1) * part_blks):
            value = segx_ref[ask_tab[2, w * node_blks + b]]
            if with_arrived:
                value = value + arrived[step - 2, b].astype(F32)
            dst[step - 1, b] = value.astype(BF16)
        rs_copy(direction, step, h).start()

    def one_round(r, _):
        scen_rows[r, scen] = risk_ref[...]
        for d in range(1, ns):
            sc_copy(r, d).start()
        piece = arc_blks // 16
        answer_group(4)
        pull_local(0, 4 * piece)
        done = 4
        for step in range(1, 4):
            for turn in range(PARTS):
                for direction in range(2):
                    h = TURNS[direction][turn]
                    ag_copy(direction, step, h).wait_recv()
                    if step < 3 or turn < PARTS // 2:
                        ag_copy(direction, step + 1, h).start()
                if turn == PARTS - 1:
                    answer_group(4 - step)
                pull_local(done * piece, piece)
                done += 1
            if step > 1:
                pull_heads(6 - step)
        for turn in range(PARTS // 2):
            for direction in range(2):
                ag_copy(direction, 4, TURNS[direction][turn]).wait_recv()
        answer_group(0)
        risk_wide = jnp.broadcast_to(
            jnp.sum(jnp.where(diagonal, jnp.broadcast_to(risk_ref[...], (rows, blk)), 0.0), axis=1, keepdims=True),
            (rows, blk),
        )
        for g in (2, 1, 0):
            pull_heads(g)

        def move(i, loss):
            js = [i * 4 + u for u in range(4)]
            pulled = [pull_ref[j] + hp_ref[own_tab[0, j]] for j in js]
            costs = [jnp.broadcast_to(cost_ref[pl.ds(j, 1), :], (rows, blk)) for j in js]
            now = [flows_ref[:, columns(j)] for j in js]
            new = [jnp.maximum(n - PRIMAL * (risk_wide * c - p), 0.0) for n, c, p in zip(now, costs, pulled)]
            bars = [2.0 * v - n for v, n in zip(new, now)]
            for j, v, bar in zip(js, new, bars):
                flows_ref[:, columns(j)] = v
                panel_ref[j] = bar.astype(BF16)
            for c, bar in zip(costs, bars):
                loss = loss + c * bar
            return loss

        loss = lax.fori_loop(0, arc_blks // 4, move, jnp.zeros((rows, blk), F32))
        keep = pltpu.make_async_copy(flows_ref, flows_out, load_sem.at[7])

        @pl.when(r == ROUNDS - 1)
        def _():
            keep.start()

        for g in range(len(GROUPS)):
            push_heads(g)
        wide = jnp.broadcast_to(jnp.sum(loss, axis=1, keepdims=True), (rows, blk))
        lossx[r, x] = jnp.sum(jnp.where(diagonal, wide, 0.0), axis=0, keepdims=True)
        for e in range(1, nx):
            lx_copy(r, e).start()
        for direction in range(2):
            for step in range(1, 5):
                for turn in range(PARTS):
                    if step < 4 or turn < PARTS // 2:
                        ag_copy(direction, step, TURNS[direction][turn]).wait_send()
        for g in range(len(GROUPS)):
            for e in range(1, nx):
                x_copy(g, e).wait_send()
        push_local(0, 4 * piece)

        for e in range(1, nx):
            f_copy(0, e).wait_recv()
        collect(0)
        for turn in range(PARTS // 2):
            for direction in range(2):
                send_sum(direction, 1, TURNS[direction][turn], False)
        for e in range(1, nx):
            lx_copy(r, e).wait_recv()
        total = lossx[r, 0]
        for i in range(1, nx):
            total = total + lossx[r, i]
        lossz[r, z] = total
        for d in range(1, NZ):
            lz_copy(r, d).start()
        done = 4
        for step in range(2, 5):
            for e in range(1, nx):
                f_copy(step - 1, e).wait_recv()
            collect(2 * step - 3)
            collect(2 * step - 2)
            for turn in range(PARTS):
                for direction in range(2):
                    send_sum(direction, step, TURNS[1 - direction][turn], step > 2 or turn >= PARTS // 2)
                push_local(done * piece, piece)
                done += 1
        for e in range(1, nx):
            f_copy(4, e).wait_recv()
        collect(7)

        for d in range(1, NZ):
            lz_copy(r, d).wait_recv()
        losses = lossz[r, 0]
        for i in range(1, NZ):
            losses = losses + lossz[r, i]
        losses = losses / arc_total
        for d in range(1, ns):
            sc_copy(r, d).wait_recv()
        risk_sum = scen_rows[r, 0]
        for i in range(1, ns):
            risk_sum = risk_sum + scen_rows[r, i]
        mean = jnp.broadcast_to(jnp.sum(risk_sum, axis=1, keepdims=True), (1, blk)) / scen_total
        risk = risk_ref[...]
        excess = excess_ref[...]
        level = level_ref[...]
        excess_new = jnp.maximum(excess - PRIMAL * (TAIL - risk), 0.0)
        level_new = level - PRIMAL * (1.0 - mean)
        excess_bar = 2.0 * excess_new - excess
        level_bar = 2.0 * level_new - level
        risk_new = jnp.maximum(risk + RISK * (losses - excess_bar - level_bar), 0.0)
        excess_ref[...] = excess_new
        level_ref[...] = level_new
        for d in range(1, ns):
            sc_copy(r, d).wait_send()
        for d in range(1, NZ):
            lz_copy(r, d).wait_send()
        for e in range(1, nx):
            lx_copy(r, e).wait_send()
        risk_ref[...] = jnp.where(real, risk_new, 0.0)

        for turn in range(PARTS):
            for direction in range(2):
                rs_copy(direction, 4, TURNS[1 - direction][turn]).wait_recv()
        for b in range(node_blks):
            pushed = (
                seg_ref[own_tab[2 + touches, b]]
                + segx_ref[ask_tab[2, 7 * node_blks + b]]
                + (ll_ref[3, b].astype(F32) + rr_ref[3, b].astype(F32))
            )
            dual = duals_ref[:, b * blk : (b + 1) * blk] + DUAL * (demand_ref[:, b * blk : (b + 1) * blk] - pushed)
            duals_ref[:, b * blk : (b + 1) * blk] = dual
            c0[b] = dual.astype(BF16)
        for direction in range(2):
            for step in range(1, 5):
                for turn in range(PARTS):
                    if step > 1 or turn < PARTS // 2:
                        rs_copy(direction, step, TURNS[direction][turn]).wait_send()
        for g in range(len(GROUPS)):
            for e in range(1, nx):
                f_copy(g, e).wait_send()

        @pl.when(r < ROUNDS - 1)
        def _():
            start_ring()

        return 0

    lax.fori_loop(0, ROUNDS, one_round, 0)
    pltpu.make_async_copy(flows_ref, flows_out, load_sem.at[7]).wait()
    excess_out[...] = excess_ref[:, 0:rows]
    risk_out[...] = risk_ref[:, 0:rows]
    level_out[...] = level_ref[:, 0:1]


def per_device(
    arc_flows,
    node_duals,
    demand,
    excess,
    risk_duals,
    threshold,
    arc_costs,
    local_blocks,
    head_blocks,
    local_index,
    head_index,
):
    blk = local_blocks.shape[-1]
    rows, arcs = arc_flows.shape
    arc_blks, touches = local_index.shape
    node_blks = node_duals.shape[1] // blk
    net = lax.axis_size("net")
    ns = lax.axis_size("scen")
    nx = net // NZ
    slots = NZ * SLOT
    smem = pl.BlockSpec(memory_space=pltpu.SMEM)
    vmem = pl.BlockSpec(memory_space=pltpu.VMEM)
    hbm = pl.BlockSpec(memory_space=pl.ANY)

    def floats(*shape):
        return jax.ShapeDtypeStruct(shape, F32)

    def panel(*lead):
        return pltpu.VMEM((*lead, rows, blk), BF16)

    def wide(*lead):
        return pltpu.VMEM((*lead, rows, blk), F32)

    def row(*lead):
        return pltpu.VMEM((*lead, 1, blk), F32)

    dma = pltpu.SemaphoreType.DMA
    groups = len(GROUPS)
    scratch = (
        [
            pltpu.VMEM(local_blocks.shape, BF16),
            pltpu.VMEM(head_blocks.shape, BF16),
            pltpu.VMEM(arc_flows.shape, F32),
            pltpu.VMEM(demand.shape, F32),
        ]
        + [panel(node_blks)] * NZ
        + [
            pltpu.VMEM((nx, nx * slots), jnp.int32),
            pltpu.SMEM((nx, nx * slots), jnp.int32),
            pltpu.SMEM((4, 128), jnp.int32),
            wide(arc_blks),
            panel(arc_blks),
            wide(arc_blks * touches + 1),
            wide(nx * slots + 1),
            wide(nx * slots),
            wide(slots),
            panel(nx * slots),
            panel(nx * slots),
            panel(nx * slots),
            panel(nx * slots),
            panel(4, node_blks),
            panel(4, node_blks),
            panel(4, node_blks),
            panel(4, node_blks),
            row(),
            row(),
            row(),
            row(ROUNDS, nx),
            row(ROUNDS, NZ),
            row(ROUNDS, ns),
            dma((8,)),
        ]
        + [dma((nx - 1,))] * 2
        + [dma((8 * PARTS,))] * 2
        + [dma((groups * (nx - 1),))] * 4
        + [dma((8 * PARTS,))] * 2
        + [dma((ROUNDS * (nx - 1),))] * 2
        + [dma((ROUNDS * (NZ - 1),))] * 2
        + [dma((ROUNDS * (ns - 1),))] * 2
    )
    own, want = pl.pallas_call(
        functools.partial(table_kernel, nx, node_blks),
        out_shape=(
            jax.ShapeDtypeStruct((8, blk), jnp.int32),
            jax.ShapeDtypeStruct((1, nx * slots), jnp.int32),
        ),
        in_specs=[vmem, vmem],
        out_specs=(vmem, vmem),
        name="tables",
    )(head_index.reshape(1, arc_blks), local_index.T)
    flows, duals, excess, risk, level = pl.pallas_call(
        functools.partial(main_kernel, nx, ns, float(rows * ns), float(arcs * net)),
        out_shape=(floats(rows, arcs), floats(*node_duals.shape), floats(1, rows), floats(1, rows), floats(1, 1)),
        in_specs=[hbm, hbm, hbm, vmem, vmem, vmem, vmem, hbm, hbm, smem, smem, vmem],
        out_specs=(hbm, vmem, vmem, vmem, vmem),
        scratch_shapes=scratch,
        compiler_params=pltpu.CompilerParams(
            collective_id=0, has_side_effects=True, vmem_limit_bytes=67043328
        ),
        name="rounds",
    )(
        node_duals,
        arc_flows,
        demand,
        arc_costs.reshape(arc_blks, blk),
        excess.reshape(1, rows),
        risk_duals.reshape(1, rows),
        threshold.reshape(1, 1),
        local_blocks,
        head_blocks,
        local_index.T,
        own,
        want,
    )
    return flows, duals, excess.reshape(-1), risk.reshape(-1), level.reshape(-1)


def solution(mesh):
    placed = (
        P("scen", "net"),
        P("scen", "net"),
        P("scen", "net"),
        P("scen"),
        P("scen"),
        P(),
        P("net"),
        P("net", None, None, None),
        P("net", None, None),
        P("net", None),
        P("net"),
    )
    return jax.shard_map(
        per_device,
        mesh=mesh,
        in_specs=placed,
        out_specs=(P("scen", "net"), P("scen", "net"), P("scen"), P("scen"), P()),
        check_vma=False,
    )
```

time: 208 us -> 161 us (0.77)
  Pallas kernels: 187 us -> 149 us
  local copies, waits for them, and re-layouts: 14.9 us -> 6.23 us
    pallas_call x1, Pallas kernels: 181 us -> 148 us  [per_device(): pl.pallas_call(functools.partial(main_kernel, nx, ns, float(rows * ns), f...]
    unnamed x31 -> x4, local copies, waits for them, and re-layouts: 14.9 us -> 6.23 us
    pallas_call x1, Pallas kernels: 6.11 us -> 1.56 us  [per_device(): pl.pallas_call(functools.partial(table_kernel, nx, node_blks), out_shape=...]
where the time goes in v2:
time: 161 us; the launch traced here: 159 us
  Pallas kernels  149 us (93%)
  local copies, waits for them, and re-layouts  6.23 us (4%)
  between operations  3.05 us (2%)
    pallas_call x1, Pallas kernels, per_device(): pl.pallas_call(functools.partial(main_kernel, nx, ns, float(rows * ns), f...  148 us
    unnamed x4, local copies, waits for them, and re-layouts  6.23 us

profile of v2, /device:TPU:0, one launch (start us, length us, event | category | flops | bytes accessed | tf_op | source)
XLA Modules:
  0.0 158.6 jit_solution(9211027065903652289)
XLA Ops:
  1.3 1.6 tables.1
  2.8 147.7 %rounds.1 = (f32[32,8192]{1,0:T(8,128)}, f32[32,2048]{1,0:T(8,128)}, f32[1,32]{1,0:T(1,128)}, f32[1,32]{1,0:T(1,128)}, f32[1,1]{1,0:T(1,128)}) custom-call(f32[32,2048]{1,0:T(8,128)} %duals_hbm.1, f32[32,8192]{1,0:T(8,128)} %flows_hbm.1, f32[32,2048]{1,0:T(8,128)} %demand_hbm.1, f32[64,128]{1,0:T(8,128)} %bitcast.10, f32[1,32]{1,0:T(1,128)} %bitcast.13, ...), custom_call_target="tpu_custom_call" | custom-call | tf_op jit(solution)/shard_map/rounds/pallas_call | solution.py:651
  150.6 2.3 %copy.22 = f32[32,8192]{1,0:T(8,128)} copy(f32[32,8192]{1,0:T(8,128)} %get-tuple-element.24) | data formatting | bytes 2097152
  152.8 1.7 %copy.23 = f32[32,2048]{1,0:T(8,128)} copy(f32[32,2048]{1,0:T(8,128)} %get-tuple-element.25) | data formatting | bytes 524288
  154.5 1.2 copy.24
  155.7 1.1 copy.25

commit v3 on v2

--- a/solution.py
+++ b/solution.py
@@ -295,16 +295,14 @@
             found = jnp.int32(0)
             for p in range(q):
                 found = jnp.where(named[p] == named[q], places[p] + 1, found)
-            ask_tab[0, i] = jnp.minimum(named[q], node_blks - 1)
-            ask_tab[1, i] = found
+            ask_tab[0, i] = found
         for b in range(node_blks):
             found = jnp.int32(0)
             for q, i in enumerate(places):
                 found = jnp.where(named[q] == b, i + 1, found)
-            ask_tab[2, w * node_blks + b] = found
+            ask_tab[1, w * node_blks + b] = found
         return 0
 
-    lax.fori_loop(0, NZ, chain_tables, 0)
     for load in loads[1:]:
         load.wait()
 
@@ -339,7 +337,8 @@
                 chunk = chunks[ORDER[w]]
                 for s in range(SLOT):
                     i = e * slots + w * SLOT + s
-                    (x_in if e == 0 else x_out)[i] = chunk[ask_tab[0, i]]
+                    named = own_tab[touches + 3, i] if e == 0 else ask_ref[e, i]
+                    (x_in if e == 0 else x_out)[i] = chunk[jnp.minimum(named, node_blks - 1)]
             if e > 0:
                 x_copy(g, e).start()
 
@@ -380,7 +379,7 @@
             i = w * SLOT + q % SLOT
             n = e * slots + i
             value = own_ref[i] if e == 0 else fx_in[n].astype(F32)
-            segx_ref[n + 1] = value + segx_ref[ask_tab[1, n]]
+            segx_ref[n + 1] = value + segx_ref[ask_tab[0, n]]
 
     def send_sum(direction, step, h, with_arrived):
         w = ORDER.index(5 - step if direction == 0 else 3 + step)
@@ -389,7 +388,7 @@
         if with_arrived:
             rs_copy(direction, step - 1, h).wait_recv()
         for b in range(h * part_blks, (h + 1) * part_blks):
-            value = segx_ref[ask_tab[2, w * node_blks + b]]
+            value = segx_ref[ask_tab[1, w * node_blks + b]]
             if with_arrived:
                 value = value + arrived[step - 2, b].astype(F32)
             dst[step - 1, b] = value.astype(BF16)
@@ -420,6 +419,11 @@
             for direction in range(2):
                 ag_copy(direction, 4, TURNS[direction][turn]).wait_recv()
         answer_group(0)
+
+        @pl.when(r == 0)
+        def _():
+            lax.fori_loop(0, NZ, chain_tables, 0)
+
         risk_wide = jnp.broadcast_to(
             jnp.sum(jnp.where(diagonal, jnp.broadcast_to(risk_ref[...], (rows, blk)), 0.0), axis=1, keepdims=True),
             (rows, blk),
@@ -492,6 +496,31 @@
         for e in range(1, nx):
             f_copy(4, e).wait_recv()
         collect(7)
+
+        for turn in range(PARTS):
+            for direction in range(2):
+                rs_copy(direction, 4, TURNS[1 - direction][turn]).wait_recv()
+        for b in range(node_blks):
+            pushed = (
+                seg_ref[own_tab[2 + touches, b]]
+                + segx_ref[ask_tab[1, 7 * node_blks + b]]
+                + (ll_ref[3, b].astype(F32) + rr_ref[3, b].astype(F32))
+            )
+            dual = duals_ref[:, b * blk : (b + 1) * blk] + DUAL * (demand_ref[:, b * blk : (b + 1) * blk] - pushed)
+            duals_ref[:, b * blk : (b + 1) * blk] = dual
+            c0[b] = dual.astype(BF16)
+        @pl.when(r < ROUNDS - 1)
+        def _():
+            start_ring()
+
+        for direction in range(2):
+            for step in range(1, 5):
+                for turn in range(PARTS):
+                    if step > 1 or turn < PARTS // 2:
+                        rs_copy(direction, step, TURNS[direction][turn]).wait_send()
+        for g in range(len(GROUPS)):
+            for e in range(1, nx):
+                f_copy(g, e).wait_send()
 
         for d in range(1, NZ):
             lz_copy(r, d).wait_recv()
@@ -522,32 +551,6 @@
         for e in range(1, nx):
             lx_copy(r, e).wait_send()
         risk_ref[...] = jnp.where(real, risk_new, 0.0)
-
-        for turn in range(PARTS):
-            for direction in range(2):
-                rs_copy(direction, 4, TURNS[1 - direction][turn]).wait_recv()
-        for b in range(node_blks):
-            pushed = (
-                seg_ref[own_tab[2 + touches, b]]
-                + segx_ref[ask_tab[2, 7 * node_blks + b]]
-                + (ll_ref[3, b].astype(F32) + rr_ref[3, b].astype(F32))
-            )
-            dual = duals_ref[:, b * blk : (b + 1) * blk] + DUAL * (demand_ref[:, b * blk : (b + 1) * blk] - pushed)
-            duals_ref[:, b * blk : (b + 1) * blk] = dual
-            c0[b] = dual.astype(BF16)
-        for direction in range(2):
-            for step in range(1, 5):
-                for turn in range(PARTS):
-                    if step > 1 or turn < PARTS // 2:
-                        rs_copy(direction, step, TURNS[direction][turn]).wait_send()
-        for g in range(len(GROUPS)):
-            for e in range(1, nx):
-                f_copy(g, e).wait_send()
-
-        @pl.when(r < ROUNDS - 1)
-        def _():
-            start_ring()
-
         return 0
 
     lax.fori_loop(0, ROUNDS, one_round, 0)
@@ -555,6 +558,11 @@
     excess_out[...] = excess_ref[:, 0:rows]
     risk_out[...] = risk_ref[:, 0:rows]
     level_out[...] = level_ref[:, 0:1]
+
+
+def finish_kernel(*refs):
+    for src, dst in zip(refs[:5], refs[5:]):
+        dst[...] = src[...]
 
 
 def per_device(
@@ -648,7 +656,7 @@
         out_specs=(vmem, vmem),
         name="tables",
     )(head_index.reshape(1, arc_blks), local_index.T)
-    flows, duals, excess, risk, level = pl.pallas_call(
+    results = pl.pallas_call(
         functools.partial(main_kernel, nx, ns, float(rows * ns), float(arcs * net)),
         out_shape=(floats(rows, arcs), floats(*node_duals.shape), floats(1, rows), floats(1, rows), floats(1, 1)),
         in_specs=[hbm, hbm, hbm, vmem, vmem, vmem, vmem, hbm, hbm, smem, smem, vmem],
@@ -672,6 +680,14 @@
         own,
         want,
     )
+    flows, duals, excess, risk, level = pl.pallas_call(
+        finish_kernel,
+        out_shape=tuple(floats(*result.shape) for result in results),
+        in_specs=[vmem] * 5,
+        out_specs=(vmem,) * 5,
+        compiler_params=pltpu.CompilerParams(vmem_limit_bytes=67043328),
+        name="finish",
+    )(*results)
     return flows, duals, excess.reshape(-1), risk.reshape(-1), level.reshape(-1)
 
 

time: 161 us -> 153 us (0.950); the launches traced: 159 us -> 152 us
  local copies, waits for them, and re-layouts: 6.23 us -> 0 us
  Pallas kernels: 149 us -> 151 us
  between operations: 3.05 us -> 1.29 us
    unnamed x4 -> x0, local copies, waits for them, and re-layouts: 6.23 us -> none
    pallas_call x0 -> x1, Pallas kernels: none -> 3.03 us  [per_device(): pl.pallas_call(finish_kernel, out_shape=tuple((floats(*result.shape) for...]
where the time goes in v3:
time: 153 us; the launch traced here: 152 us
  Pallas kernels  151 us (99%)
    pallas_call x1, Pallas kernels, per_device(): pl.pallas_call(functools.partial(main_kernel, nx, ns, float(rows * ns), f...  146 us

profile of v3, /device:TPU:0, one launch (start us, length us, event | category | flops | bytes accessed | tf_op | source)
XLA Modules:
  0.0 152.3 jit_solution(12658865771982659157)
XLA Ops:
  1.3 1.6 %tables.1 = (s32[8,128]{1,0:T(8,128)}, s32[1,128]{1,0:T(1,128)}) custom-call(s32[1,64]{1,0:T(1,128)} %bitcast.15, s32[4,64]{1,0:T(4,128)} %bitcast.11), custom_call_target="tpu_custom_call" | custom-call | tf_op jit(solution)/shard_map/tables/pallas_call | solution.py:649
  2.8 146.4 %rounds.1 = (f32[32,8192]{1,0:T(8,128)}, f32[32,2048]{1,0:T(8,128)}, f32[1,32]{1,0:T(1,128)}, f32[1,32]{1,0:T(1,128)}, f32[1,1]{1,0:T(1,128)}) custom-call(f32[32,2048]{1,0:T(8,128)} %duals_hbm.1, f32[32,8192]{1,0:T(8,128)} %flows_hbm.1, f32[32,2048]{1,0:T(8,128)} %demand_hbm.1, f32[64,128]{1,0:T(8,128)} %bitcast.10, f32[1,32]{1,0:T(1,128)} %bitcast.13, ...), custom_call_target="tpu_custom_call" | custom-call | tf_op jit(solution)/shard_map/rounds/pallas_call | solution.py:659
  149.2 3.0 %finish.1 = (f32[32,8192]{1,0:T(8,128)}, f32[32,2048]{1,0:T(8,128)}, f32[1,32]{1,0:T(1,128)}, f32[1,32]{1,0:T(1,128)}, f32[1,1]{1,0:T(1,128)}) custom-call(f32[32,8192]{1,0:T(8,128)} %get-tuple-element.19.refs_0_, f32[32,2048]{1,0:T(8,128)} %get-tuple-element.20.refs_1_, f32[1,32]{1,0:T(1,128)} %get-tuple-element.21.refs_2_, ...), custom_call_target="tpu_custom_call" | custom-call | tf_op jit(solution)/shard_map/finish/pallas_call | solution.py:683

commit v4 on v3

--- a/solution.py
+++ b/solution.py
@@ -317,7 +317,7 @@
             pull_ref[j] = total
             return 0
 
-        lax.fori_loop(0, count, body, 0, unroll=4)
+        lax.fori_loop(0, count, body, 0, unroll=min(4, count))
 
     def push_local(first, count):
         def body(i, _):
@@ -328,7 +328,7 @@
                 seg_ref[j * touches + k + 1] = term + seg_ref[own_tab[2 + k, j]]
             return 0
 
-        lax.fori_loop(0, count, body, 0, unroll=4)
+        lax.fori_loop(0, count, body, 0, unroll=min(4, count))
 
     def answer_group(g):
         first, count = GROUPS[g]
@@ -353,7 +353,7 @@
 
         for e in range(1, nx):
             x_copy(g, e).wait_recv()
-        lax.fori_loop(0, nx, body, 0)
+        lax.fori_loop(0, nx, body, 0, unroll=nx if g == 0 else 1)
 
     def push_heads(g):
         first, count = GROUPS[g]
@@ -367,7 +367,7 @@
                 fx_out[e * slots + first * SLOT + s] = term(e, s).astype(BF16)
             return 0
 
-        lax.fori_loop(1, nx, body, 0)
+        lax.fori_loop(1, nx, body, 0, unroll=nx - 1 if g == 0 else 1)
         for e in range(1, nx):
             f_copy(g, e).start()
         for s in range(count * SLOT):
@@ -398,10 +398,12 @@
         scen_rows[r, scen] = risk_ref[...]
         for d in range(1, ns):
             sc_copy(r, d).start()
-        piece = arc_blks // 16
+        piece = arc_blks // 32
+        ahead = (arc_blks - 12 * piece) // 2
+        after = arc_blks - 12 * piece - ahead
         answer_group(4)
-        pull_local(0, 4 * piece)
-        done = 4
+        pull_local(0, ahead)
+        done = ahead
         for step in range(1, 4):
             for turn in range(PARTS):
                 for direction in range(2):
@@ -411,8 +413,8 @@
                         ag_copy(direction, step + 1, h).start()
                 if turn == PARTS - 1:
                     answer_group(4 - step)
-                pull_local(done * piece, piece)
-                done += 1
+                pull_local(done, piece)
+                done += piece
             if step > 1:
                 pull_heads(6 - step)
         for turn in range(PARTS // 2):
@@ -424,6 +426,7 @@
         def _():
             lax.fori_loop(0, NZ, chain_tables, 0)
 
+        pull_local(done, after)
         risk_wide = jnp.broadcast_to(
             jnp.sum(jnp.where(diagonal, jnp.broadcast_to(risk_ref[...], (rows, blk)), 0.0), axis=1, keepdims=True),
             (rows, blk),
@@ -466,7 +469,7 @@
         for g in range(len(GROUPS)):
             for e in range(1, nx):
                 x_copy(g, e).wait_send()
-        push_local(0, 4 * piece)
+        push_local(0, ahead)
 
         for e in range(1, nx):
             f_copy(0, e).wait_recv()
@@ -482,7 +485,7 @@
         lossz[r, z] = total
         for d in range(1, NZ):
             lz_copy(r, d).start()
-        done = 4
+        done = ahead
         for step in range(2, 5):
             for e in range(1, nx):
                 f_copy(step - 1, e).wait_recv()
@@ -491,11 +494,12 @@
             for turn in range(PARTS):
                 for direction in range(2):
                     send_sum(direction, step, TURNS[1 - direction][turn], step > 2 or turn >= PARTS // 2)
-                push_local(done * piece, piece)
-                done += 1
+                push_local(done, piece)
+                done += piece
         for e in range(1, nx):
             f_copy(4, e).wait_recv()
         collect(7)
+        push_local(done, after)
 
         for turn in range(PARTS):
             for direction in range(2):

time: 153 us -> 153 us (level)
  no operation moved by 1% of the time
where the time goes in v4:
time: 153 us; the launch traced here: 152 us
  Pallas kernels  151 us (99%)
    pallas_call x1, Pallas kernels, per_device(): pl.pallas_call(functools.partial(main_kernel, nx, ns, float(rows * ns), f...  146 us

profile of v4, /device:TPU:0, one launch (start us, length us, event | category | flops | bytes accessed | tf_op | source)
XLA Modules:
  0.0 152.1 jit_solution(7119276620734966995)
XLA Ops:
  1.3 1.6 %tables.1 = (s32[8,128]{1,0:T(8,128)}, s32[1,128]{1,0:T(1,128)}) custom-call(s32[1,64]{1,0:T(1,128)} %bitcast.15, s32[4,64]{1,0:T(4,128)} %bitcast.11), custom_call_target="tpu_custom_call" | custom-call | tf_op jit(solution)/shard_map/tables/pallas_call | solution.py:653
  2.8 146.2 %rounds.1 = (f32[32,8192]{1,0:T(8,128)}, f32[32,2048]{1,0:T(8,128)}, f32[1,32]{1,0:T(1,128)}, f32[1,32]{1,0:T(1,128)}, f32[1,1]{1,0:T(1,128)}) custom-call(f32[32,2048]{1,0:T(8,128)} %duals_hbm.1, f32[32,8192]{1,0:T(8,128)} %flows_hbm.1, f32[32,2048]{1,0:T(8,128)} %demand_hbm.1, f32[64,128]{1,0:T(8,128)} %bitcast.10, f32[1,32]{1,0:T(1,128)} %bitcast.13, ...), custom_call_target="tpu_custom_call" | custom-call | tf_op jit(solution)/shard_map/rounds/pallas_call | solution.py:663
  149.1 3.0 %finish.1 = (f32[32,8192]{1,0:T(8,128)}, f32[32,2048]{1,0:T(8,128)}, f32[1,32]{1,0:T(1,128)}, f32[1,32]{1,0:T(1,128)}, f32[1,1]{1,0:T(1,128)}) custom-call(f32[32,8192]{1,0:T(8,128)} %get-tuple-element.19.refs_0_, f32[32,2048]{1,0:T(8,128)} %get-tuple-element.20.refs_1_, f32[1,32]{1,0:T(1,128)} %get-tuple-element.21.refs_2_, ...), custom_call_target="tpu_custom_call" | custom-call | tf_op jit(solution)/shard_map/finish/pallas_call | solution.py:687
